TPU v7x, 128 devices: a whole 4x4x4 slice. The times are simulated.
128 devices in a mesh: sub: 8 (over z, core), grp: 16 (over x, y).
Axes of the slice: x: 4, y: 4, z: 4, core: 2. Of those that a mesh axis runs over, the one named last changes fastest.
Arguments:
- schur: bfloat16 [512, 1024, 1024], P(('sub', 'grp')), as said below
- mortar: bfloat16 [512, 8, 128, 128], P(('sub', 'grp')), may hold values from -0.5 to 0.5
- partner: int32 [512, 4], P(('sub', 'grp')), may hold values from 0 to 15, as said below
- corner_map: int32 [512, 8], P(('sub', 'grp')), may hold values from 0 to 127
- coarse_inv: float32 [8, 128, 128], P('sub'), as said below
- load: float32 [512, 1024, 384], P(('sub', 'grp')), may hold values from -6 to 6
Outputs:
- solution: float32 [512, 1024, 384], P(('sub', 'grp'))
Inputs may be any that keep to these rules, and one draw needn't show every extreme that they name: `partner`: within the 4 subdomains of one device, the entries form a permutation of 0 to 15. `schur`: each matrix is symmetric positive definite. `coarse_inv`: each matrix is symmetric positive definite.
All inputs are finite; a program needn't handle non-finite values.
Results may differ from a plain program's by a relative error of at most 0.0025.
Values may be sent and summed in bfloat16 or wider, within the bound.
A program may use at most 128 MiB of HBM per device.

v0:
```python
import jax
import jax.numpy as jnp
from jax import lax
from jax.sharding import PartitionSpec as P

ITERS = 2


def shifted(block, axis, distance):
    devices = range(lax.axis_size(axis))
    route = [((i - distance) % len(devices), i) for i in devices]
    return lax.ppermute(block, axis, route)


def face_terms(direction, schur, mortar, partner):
    subdoms = direction.shape[0]
    order = direction.shape[1]
    columns = direction.shape[2]
    faces_all = mortar.shape[1]
    block = mortar.shape[2]
    half_faces = faces_all // 2
    dir_half = direction.astype(jnp.bfloat16)
    stiff = jnp.einsum("sij,sjr->sir", schur, dir_half, preferred_element_type=jnp.float32)
    face_rows = dir_half.reshape(subdoms, faces_all, block, columns)
    traces = jnp.einsum(
        "sfij,sfjr->sfir", mortar, face_rows, preferred_element_type=jnp.float32
    ).astype(jnp.bfloat16)
    upper = traces[:, :half_faces].reshape(subdoms * half_faces, block, columns)
    lower = traces[:, half_faces:].reshape(subdoms * half_faces, block, columns)
    mates = partner.reshape(-1)
    inverse = jnp.argsort(mates)
    reordered = jnp.take(upper, inverse, axis=0)
    lower_mate = shifted(reordered, "sub", 1)
    jump_lower = (lower.astype(jnp.float32) - lower_mate.astype(jnp.float32)).astype(jnp.bfloat16)
    above = shifted(lower, "sub", -1)
    upper_mate = jnp.take(above, mates, axis=0)
    jump_upper = (upper.astype(jnp.float32) - upper_mate.astype(jnp.float32)).astype(jnp.bfloat16)
    jump_all = jnp.concatenate(
        [
            jump_upper.reshape(subdoms, half_faces, block, columns),
            jump_lower.reshape(subdoms, half_faces, block, columns),
        ],
        axis=1,
    )
    pulled = jnp.einsum("sfji,sfjr->sfir", mortar, jump_all, preferred_element_type=jnp.float32)
    return stiff + pulled.reshape(subdoms, order, columns)


def squares(residual):
    return lax.psum(jnp.sum(residual * residual, axis=(0, 1)), ("sub", "grp"))


def on_device(schur, mortar, partner, corner_map, coarse_inv, load):
    order = load.shape[1]
    corner_count = corner_map.shape[1]
    coarse_count = coarse_inv.shape[1]
    stride = order // corner_count
    onehot = (corner_map[..., None] == jnp.arange(coarse_count, dtype=jnp.int32)).astype(
        jnp.float32
    )
    coarse_matrix = coarse_inv[0]
    solution = jnp.zeros_like(load)
    residual = load
    direction = load
    norm_now = squares(residual)
    for step in range(ITERS):
        partial_value = face_terms(direction, schur, mortar, partner)
        corners = direction[:, ::stride, :]
        local_sum = jnp.einsum("sco,scr->or", onehot, corners, precision=lax.Precision.HIGHEST)
        coarse_sum = lax.psum(local_sum.astype(jnp.bfloat16), "grp").astype(jnp.float32)
        coarse_val = jnp.dot(coarse_matrix, coarse_sum, precision=lax.Precision.HIGHEST)
        corner_add = jnp.einsum("sco,or->scr", onehot, coarse_val, precision=lax.Precision.HIGHEST)
        image = partial_value.at[:, ::stride, :].add(corner_add)
        curvature = lax.psum(jnp.sum(direction * image, axis=(0, 1)), ("sub", "grp"))
        image, curvature = (image, curvature)
        step_len = norm_now / curvature
        solution = solution + step_len * direction
        if step + 1 < ITERS:
            residual = residual - step_len * image
            norm_next = squares(residual)
            direction = residual + norm_next / norm_now * direction
            norm_now = norm_next
    return solution


def solution(mesh):
    return jax.shard_map(
        on_device,
        mesh=mesh,
        in_specs=(
            P(("sub", "grp"), None, None),
            P(("sub", "grp"), None, None, None),
            P(("sub", "grp"), None),
            P(("sub", "grp"), None),
            P("sub", None, None),
            P(("sub", "grp"), None, None),
        ),
        out_specs=P(("sub", "grp"), None, None),
        check_vma=False,
    )
```

profile of v0, /device:TPU:1, one launch (start us, length us, event | category | flops | bytes accessed | tf_op | source)
XLA Modules:
  0.0 520.1 jit_solution(5917532602240920158)
XLA Ops:
  6.5 5.6 %multiply_reduce_fusion.1 = (f32[384]{0:T(512)S(1)}, bf16[4,1024,384]{2,1,0:T(8,128)(2,1)S(1)}) fusion(f32[4,1024,384]{2,1,0:T(8,128)} %param.13), kind=kLoop, calls=%fused_computation.17 | loop fusion | flops 4718208 | bytes 9438720 | tf_op jit(solution)/shard_map/reduce_sum | solution.py:50
  12.2 1.0 convolution_convert_fusion
  13.8 1.5 fusion.23
  15.4 1.4 collective-permute-start
  16.9 1.2 sort.19
  18.1 1.9 gather_fusion.1
  20.0 2.8 broadcast_select_fusion.1
  22.8 1.6 collective-permute-start.1
  24.4 2.8 slice.20
  27.3 1.0 fusion.11
  28.6 82.6 %all-reduce.4.cloned.1.call-done = bf16[128,384]{1,0:T(8,128)(2,1)} async-done(((bf16[128,384]{1,0:T(8,128)(2,1)}), bf16[128,384]{1,0:T(8,128)(2,1)}) %all-reduce.4.cloned.1.call-update) | async-done | bytes 98320 | tf_op jit(solution)/shard_map/psum | solution.py:70
  111.2 1.2 convolution_bitcast_fusion.1
  112.7 3.3 gather_fusion
  116.0 2.1 subtract_convert_fusion.3
  118.2 2.5 subtract_convert_fusion.2
  120.7 1.0 fusion.3
  121.8 1.3 slice-done.1
  123.0 0.9 copy-done.2
  123.9 6.9 %bitcast_add_fusion = f32[4,1024,384]{2,1,0:T(8,128)} fusion(f32[4,8,384,128]{2,3,1,0:T(8,128)S(1)} %fusion.3, bf16[4,1024,1024]{2,1,0:T(8,128)(2,1)S(1)} %bitcast.65, bf16[4,1024,384]{2,1,0:T(8,128)(2,1)S(1)} %copy-done.2), kind=kOutput, calls=%fused_computation.6 | convolution fusion | flops 3222798336 | bytes 24117248 | tf_op jit(solution)/shard_map/sij,sjr->sir/dot_general | solution.py:23
  130.8 9.5 %copy.24 = f32[4,1024,384]{2,0,1:T(4,128)} copy(f32[4,1024,384]{2,1,0:T(8,128)} %bitcast_add_fusion) | data formatting | bytes 12582912 | tf_op jit(solution)/shard_map/add | solution.py:46
  140.3 2.1 scatter_fusion
  142.4 9.6 %fusion.2 = f32[384]{0:T(512)S(1)} fusion(f32[4,1024,384]{2,0,1:T(4,128)} %scatter_fusion, f32[4,1024,384]{2,1,0:T(8,128)} %param.13), kind=kLoop, calls=%fused_computation.13 | loop fusion | flops 3145344 | bytes 12584448 | tf_op jit(solution)/shard_map/reduce_sum | solution.py:74
  152.0 64.9 %all-reduce = (f32[384]{0:T(512)S(1)}, f32[384]{0:T(512)S(1)}) all-reduce(f32[384]{0:T(512)S(1)} %get-tuple-element.12, f32[384]{0:T(512)S(1)} %fusion.2), channel_id=1, replica_groups=mesh['sub'=8,'grp'=16] {'sub','grp'}, use_global_device_ids=true, to_apply=%region_1.0 | all-reduce | flops 768 | bytes 6144 | tf_op jit(solution)/shard_map/psum | solution.py:50
  216.9 5.5 %multiply_reduce_fusion = f32[384]{0:T(512)S(1)} fusion(f32[4,1024,384]{2,1,0:T(8,128)} %param.13, f32[4,1024,384]{2,0,1:T(4,128)} %scatter_fusion, f32[384]{0:T(512)S(1)} %div.9), kind=kLoop, calls=%fused_computation.16 | loop fusion | flops 6291072 | bytes 12585984 | tf_op jit(solution)/shard_map/reduce_sum | solution.py:50
  222.4 64.4 %psum.45 = f32[384]{0:T(512)S(1)} all-reduce(f32[384]{0:T(512)S(1)} %multiply_reduce_fusion), channel_id=1, replica_groups=mesh['sub'=8,'grp'=16] {'sub','grp'}, use_global_device_ids=true, to_apply=%region_8.10 | all-reduce | flops 384 | bytes 3072 | tf_op jit(solution)/shard_map/psum | solution.py:50
  286.8 7.1 %fusion.21 = (bf16[4,1024,384]{2,1,0:T(8,128)(2,1)S(1)}, f32[4,1024,384]{2,1,0:T(8,128)}) fusion(f32[4,1024,384]{2,1,0:T(8,128)} %param.13, f32[384]{0:T(512)S(1)} %div.10, f32[4,1024,384]{2,0,1:T(4,128)} %scatter_fusion, f32[384]{0:T(512)S(1)} %div.9), kind=kLoop, calls=%fused_computation.58 | loop fusion | flops 7864320 | bytes 22023168 | tf_op jit(solution)/shard_map/convert_element_type | solution.py:22
  293.9 1.1 convert_bitcast_fusion
  295.6 1.4 fusion.22
  297.0 1.9 gather_fusion.3
  298.9 2.8 broadcast_select_fusion
  301.7 1.0 collective-permute-start.2
  302.7 2.8 slice.23
  305.5 1.0 fusion.12
  306.5 78.2 %all-reduce.6.cloned.1.call-done = bf16[128,384]{1,0:T(8,128)(2,1)} async-done(((bf16[128,384]{1,0:T(8,128)(2,1)}), bf16[128,384]{1,0:T(8,128)(2,1)}) %all-reduce.6.cloned.1.call-update) | async-done | bytes 98320 | tf_op jit(solution)/shard_map/psum | solution.py:70
  384.7 1.2 convolution_bitcast_fusion
  386.1 3.5 subtract_convert_fusion
  389.6 2.6 copy.31
  392.2 3.3 gather_fusion.2
  395.5 3.1 subtract_convert_fusion.1
  398.7 2.7 copy.30
  401.3 5.1 fusion.7
  406.4 6.5 %copy.41 = f32[4,1024,384]{1,2,0:T(8,128)} copy(f32[4,1024,384]{2,1,0:T(8,128)} %bitcast.68) | data formatting | bytes 12582912 | tf_op jit(solution)/shard_map/reshape | solution.py:46
  413.0 12.4 %bitcast_add_fusion.1 = f32[4,1024,384]{1,2,0:T(8,128)} fusion(f32[4,1024,384]{1,2,0:T(8,128)} %copy.41, bf16[4,1024,384]{2,1,0:T(8,128)(2,1)} %copy-done.3, bf16[4,1024,1024]{2,1,0:T(8,128)(2,1)} %param.8), kind=kOutput, calls=%fused_computation.7 | convolution fusion | flops 3222798336 | bytes 24117248 | tf_op jit(solution)/shard_map/sij,sjr->sir/dot_general | solution.py:23
  425.3 7.7 %copy.34 = f32[4,1024,384]{2,0,1:T(4,128)} copy(f32[4,1024,384]{1,2,0:T(8,128)} %bitcast_add_fusion.1) | data formatting | bytes 12582912 | tf_op jit(solution)/shard_map/add | solution.py:46
  433.0 2.1 scatter_fusion.1
  435.1 5.3 %fusion = f32[384]{0:T(512)S(1)} fusion(f32[4,1024,384]{2,1,0:T(8,128)} %get-tuple-element.11, f32[4,1024,384]{2,0,1:T(4,128)} %scatter_fusion.1), kind=kLoop, calls=%fused_computation.9 | loop fusion | flops 3145344 | bytes 12584448 | tf_op jit(solution)/shard_map/reduce_sum | solution.py:74
  440.3 64.9 %psum.47 = f32[384]{0:T(512)S(1)} all-reduce(f32[384]{0:T(512)S(1)} %fusion), channel_id=1, replica_groups=mesh['sub'=8,'grp'=16] {'sub','grp'}, use_global_device_ids=true, to_apply=%region_12.14 | all-reduce | flops 384 | bytes 3072 | tf_op jit(solution)/shard_map/psum | solution.py:74
  505.2 8.0 %multiply_add_fusion = f32[4,1024,384]{2,1,0:T(8,128)} fusion(f32[4,1024,384]{2,1,0:T(8,128)} %get-tuple-element.11, f32[4,1024,384]{2,1,0:T(8,128)} %param.13, f32[384]{0:T(512)S(1)} %div.11, f32[384]{0:T(512)S(1)} %div.9), kind=kLoop, calls=%fused_computation.14 | loop fusion | flops 4718592 | bytes 18877440 | tf_op jit(solution)/shard_map/add | solution.py:77
  (44 shorter events, 2.3 us)
Async XLA Ops:
  6.5 5.6 %copy-start = (bf16[4,8,128,128]{3,2,1,0:T(8,128)(2,1)S(1)}, bf16[4,8,128,128]{3,2,1,0:T(8,128)(2,1)}, u32[]{:S(2)}) copy-start(bf16[4,8,128,128]{3,2,1,0:T(8,128)(2,1)} %param.9) | copy-start | bytes 3145732
  6.5 104.7 %all-reduce.4.cloned.1.call-start = ((), (), s32[]{:S(2)}) async-start(), calls=%async_computation | async-start | bytes 196608 | tf_op jit(solution)/shard_map/psum | solution.py:70
  12.2 1.7 copy-start.1
  13.8 3.0 copy-start.7
  15.4 97.3 %collective-permute-start = (bf16[16,128,384]{2,1,0:T(8,128)(2,1)}, bf16[16,128,384]{2,1,0:T(8,128)(2,1)}, u32[]{:S(2)}, u32[]{:S(2)}) collective-permute-start(bf16[16,128,384]{2,1,0:T(8,128)(2,1)} %bitcast.2), channel_id=1, source_target_pairs={{16,0},{32,16},{48,32},{64,48},{80,64},{96,80},{112,96},{0,112},{1... | collective-permute-start | bytes 4718600 | tf_op jit(solution)/shard_map/ppermute | solution.py:12
  18.1 9.2 %copy-start.6 = (s32[4,8]{1,0:T(4,128)S(1)}, s32[4,8]{1,0:T(4,128)}, u32[]{:S(2)}) copy-start(s32[4,8]{1,0:T(4,128)} %param.11) | copy-start | bytes 388
  18.1 93.1 %copy-start.5 = (f32[1,128,128]{2,1,0:T(8,128)S(1)}, f32[1,128,128]{2,1,0:T(8,128)}, u32[]{:S(2)}) copy-start(f32[1,128,128]{2,1,0:T(8,128)} %param.12) | copy-start | bytes 196612
  22.8 95.3 %collective-permute-start.1 = (bf16[16,128,384]{2,1,0:T(8,128)(2,1)}, bf16[16,128,384]{2,1,0:T(8,128)(2,1)}, u32[]{:S(2)}, u32[]{:S(2)}) collective-permute-start(bf16[16,128,384]{2,1,0:T(8,128)(2,1)} %broadcast_select_fusion.1), channel_id=1, source_target_pairs={{112,0},{0,16},{16,32},{32,48},{48,64},{64,80},{80,96},{96,112},{1... | collective-permute-start | bytes 4718600 | tf_op jit(solution)/shard_map/ppermute | solution.py:12
  28.3 356.4 %all-reduce.6.cloned.1.call-start = ((), (), s32[]{:S(2)}) async-start(), calls=%async_computation.1 | async-start | bytes 196608 | tf_op jit(solution)/shard_map/psum | solution.py:70
  118.2 3.6 slice-start
  120.7 2.3 slice-start.1
  120.7 3.2 copy-start.2
  293.9 1.7 copy-start.3
  301.7 84.4 %collective-permute-start.3 = (bf16[16,128,384]{1,2,0:T(8,128)(2,1)}, bf16[16,128,384]{1,2,0:T(8,128)(2,1)}, u32[]{:S(2)}, u32[]{:S(2)}) collective-permute-start(bf16[16,128,384]{1,2,0:T(8,128)(2,1)} %broadcast_select_fusion), channel_id=1, source_target_pairs={{112,0},{0,16},{16,32},{32,48},{48,64},{64,80},{80,96},{96,112},{1... | collective-permute-start | bytes 4718600 | tf_op jit(solution)/shard_map/ppermute | solution.py:12
  301.7 90.5 %collective-permute-start.2 = (bf16[16,128,384]{1,2,0:T(8,128)(2,1)}, bf16[16,128,384]{1,2,0:T(8,128)(2,1)}, u32[]{:S(2)}, u32[]{:S(2)}) collective-permute-start(bf16[16,128,384]{1,2,0:T(8,128)(2,1)} %bitcast.16), channel_id=1, source_target_pairs={{16,0},{32,16},{48,32},{64,48},{80,64},{96,80},{112,96},{0,112},{1... | collective-permute-start | bytes 4718600 | tf_op jit(solution)/shard_map/ppermute | solution.py:12
  398.7 2.7 copy-start.4
Sparse Core Ops, SparseCore 0:
  28.4 82.7 all-reduce.3
  306.6 77.9 all-reduce.5
where the time goes:
time: 521 us; the launch traced here: 520 us
  blocking collectives  194 us (37%)
  waiting for transfers between devices  161 us (31%)
  other arithmetic  63.4 us (12%)
  local copies, waits for them, and re-layouts  51.5 us (10%)
  matrix products  32.3 us (6%)
  between operations  13.6 us (3%)
    psum x2, waiting for transfers between devices, on_device(): lax.psum(local_sum.astype(jnp.bfloat16), 'grp').astype(jnp.float32)  161 us
    psum x2, blocking collectives, squares(): return lax.psum(jnp.sum(residual * residual, axis=(0, 1)), ('sub', 'grp'))  129 us
    psum x1, blocking collectives, on_device(): lax.psum(jnp.sum(direction * image, axis=(0, 1)), ('sub', 'grp'))  64.9 us
    dot_general x2, matrix products, face_terms(): jnp.einsum('sij,sjr->sir', schur, dir_half, preferred_element_type=jnp.fl...  19.3 us
    add x2, local copies, waits for them, and re-layouts, face_terms(): return stiff + pulled.reshape(subdoms, order, columns)  17.1 us
    reduce_sum x2, other arithmetic, on_device(): jnp.sum(direction * image, axis=(0, 1))  14.9 us
    reduce_sum x2, other arithmetic, squares(): return lax.psum(jnp.sum(residual * residual, axis=(0, 1)), ('sub', 'grp'))  11.1 us
  transfers between devices with their start and end apart: 6, of which 2 were waited for; matrix products, arithmetic and copies ran while one was open for 5% of the time, Pallas kernels for 0%

commit v1 on v0

--- a/solution.py
+++ b/solution.py
@@ -71,7 +71,7 @@
         coarse_val = jnp.dot(coarse_matrix, coarse_sum, precision=lax.Precision.HIGHEST)
         corner_add = jnp.einsum("sco,or->scr", onehot, coarse_val, precision=lax.Precision.HIGHEST)
         image = partial_value.at[:, ::stride, :].add(corner_add)
-        curvature = lax.psum(jnp.sum(direction * image, axis=(0, 1)), ("sub", "grp"))
+        curvature = lax.psum(lax.psum(jnp.sum(direction * image, axis=(0, 1)), "sub"), "grp")
         image, curvature = (image, curvature)
         step_len = norm_now / curvature
         solution = solution + step_len * direction

time: 521 us -> 494 us (0.948); the launches traced: 520 us -> 486 us
  waiting for transfers between devices: 161 us -> 85.9 us
  blocking collectives: 194 us -> 236 us
    psum x2, waiting for transfers between devices: 161 us -> 85.9 us  [on_device(): lax.psum(local_sum.astype(jnp.bfloat16), 'grp').astype(jnp.float32)]
    psum x1 -> x4, blocking collectives: 64.9 us -> 90.9 us  [the longest x2 62.1 us: on_device(): lax.psum(lax.psum(jnp.sum(direction * image, axis=(0, 1)), 'sub'), 'grp')]
    psum x2, blocking collectives: 129 us -> 145 us  [squares(): return lax.psum(jnp.sum(residual * residual, axis=(0, 1)), ('sub', 'grp'))]
  transfers between devices with their start and end apart: 6 -> 6, of which waited for: 2 -> 2; matrix products, arithmetic and copies ran while one was open for 5% -> 6% of each run, Pallas kernels for 0% -> 0%
where the time goes in v1:
time: 494 us; the launch traced here: 486 us
  blocking collectives  236 us (48%)
  waiting for transfers between devices  85.9 us (17%)
  other arithmetic  63.4 us (13%)
  local copies, waits for them, and re-layouts  51.5 us (10%)
  matrix products  32.3 us (7%)
  between operations  13.6 us (3%)
    psum x2, blocking collectives, squares(): return lax.psum(jnp.sum(residual * residual, axis=(0, 1)), ('sub', 'grp'))  145 us
    psum x2, waiting for transfers between devices, on_device(): lax.psum(local_sum.astype(jnp.bfloat16), 'grp').astype(jnp.float32)  85.9 us
    psum x2, blocking collectives, on_device(): lax.psum(lax.psum(jnp.sum(direction * image, axis=(0, 1)), 'sub'), 'grp')  62.1 us
    psum x2, blocking collectives, on_device(): lax.psum(jnp.sum(direction * image, axis=(0, 1)), 'sub')  28.8 us
    dot_general x2, matrix products, face_terms(): jnp.einsum('sij,sjr->sir', schur, dir_half, preferred_element_type=jnp.fl...  19.3 us
    add x2, local copies, waits for them, and re-layouts, face_terms(): return stiff + pulled.reshape(subdoms, order, columns)  17.1 us
    reduce_sum x2, other arithmetic, on_device(): jnp.sum(direction * image, axis=(0, 1))  14.9 us
    reduce_sum x2, other arithmetic, squares(): return lax.psum(jnp.sum(residual * residual, axis=(0, 1)), ('sub', 'grp'))  11.1 us
  transfers between devices with their start and end apart: 6, of which 2 were waited for; matrix products, arithmetic and copies ran while one was open for 6% of the time, Pallas kernels for 0%

profile of v1, /device:TPU:1, one launch (start us, length us, event | category | flops | bytes accessed | tf_op | source)
XLA Modules:
  0.0 486.5 jit_solution(17034761161365927537)
XLA Ops:
  6.5 5.6 %multiply_reduce_fusion.1 = (f32[384]{0:T(512)S(1)}, bf16[4,1024,384]{2,1,0:T(8,128)(2,1)S(1)}) fusion(f32[4,1024,384]{2,1,0:T(8,128)} %param.13), kind=kLoop, calls=%fused_computation.17 | loop fusion | flops 4718208 | bytes 9438720 | tf_op jit(solution)/shard_map/reduce_sum | solution.py:50
  12.2 1.0 convolution_convert_fusion
  13.8 1.5 fusion.23
  15.4 1.4 collective-permute-start
  16.9 1.2 sort.19
  18.1 1.9 gather_fusion.1
  20.0 2.8 broadcast_select_fusion.1
  22.8 1.6 collective-permute-start.1
  24.4 2.8 slice.20
  28.3 75.0 %psum.56 = f32[384]{0:T(512)S(1)} all-reduce(f32[384]{0:T(512)S(1)} %get-tuple-element.10), channel_id=1, replica_groups=mesh['sub'=8,'grp'=16] {'sub','grp'}, use_global_device_ids=true, to_apply=%region_1.0 | all-reduce | flops 384 | bytes 3072 | tf_op jit(solution)/shard_map/psum | solution.py:50
  103.4 7.8 %all-reduce.3.cloned.1.call-done = bf16[128,384]{1,0:T(8,128)(2,1)} async-done(((bf16[128,384]{1,0:T(8,128)(2,1)}), bf16[128,384]{1,0:T(8,128)(2,1)}) %all-reduce.3.cloned.1.call-update) | async-done | bytes 98320 | tf_op jit(solution)/shard_map/psum | solution.py:70
  111.2 1.2 convolution_bitcast_fusion.1
  112.7 3.3 gather_fusion
  116.1 2.1 subtract_convert_fusion.3
  118.2 2.5 subtract_convert_fusion.2
  120.7 1.0 fusion.3
  121.8 1.3 slice-done.1
  124.0 6.9 %bitcast_add_fusion = f32[4,1024,384]{2,1,0:T(8,128)} fusion(f32[4,8,384,128]{2,3,1,0:T(8,128)S(1)} %fusion.3, bf16[4,1024,1024]{2,1,0:T(8,128)(2,1)S(1)} %bitcast.65, bf16[4,1024,384]{2,1,0:T(8,128)(2,1)S(1)} %copy-done.2), kind=kOutput, calls=%fused_computation.6 | convolution fusion | flops 3222798336 | bytes 24117248 | tf_op jit(solution)/shard_map/sij,sjr->sir/dot_general | solution.py:23
  130.9 9.5 %copy.24 = f32[4,1024,384]{2,0,1:T(4,128)} copy(f32[4,1024,384]{2,1,0:T(8,128)} %bitcast_add_fusion) | data formatting | bytes 12582912 | tf_op jit(solution)/shard_map/add | solution.py:46
  140.4 2.1 scatter_fusion
  142.4 9.6 %fusion.2 = f32[384]{0:T(512)S(1)} fusion(f32[4,1024,384]{2,0,1:T(4,128)} %scatter_fusion, f32[4,1024,384]{2,1,0:T(8,128)} %param.13), kind=kLoop, calls=%fused_computation.13 | loop fusion | flops 3145344 | bytes 12584448 | tf_op jit(solution)/shard_map/reduce_sum | solution.py:74
  152.0 14.4 %psum.58 = f32[384]{0:T(512)S(1)} all-reduce(f32[384]{0:T(512)S(1)} %fusion.2), channel_id=1, replica_groups=mesh['sub'=8,'grp'=16] {'sub'}, use_global_device_ids=true, to_apply=%region_6.8 | all-reduce | flops 384 | bytes 3072 | tf_op jit(solution)/shard_map/psum | solution.py:74
  166.5 31.0 %psum.59 = f32[384]{0:T(512)S(1)} all-reduce(f32[384]{0:T(512)S(1)} %psum.58), channel_id=1, replica_groups=mesh['sub'=8,'grp'=16] {'grp'}, use_global_device_ids=true, to_apply=%region_7.9 | all-reduce | flops 384 | bytes 3072 | tf_op jit(solution)/shard_map/psum | solution.py:74
  197.5 5.5 %multiply_reduce_fusion = f32[384]{0:T(512)S(1)} fusion(f32[4,1024,384]{2,1,0:T(8,128)} %param.13, f32[4,1024,384]{2,0,1:T(4,128)} %scatter_fusion, f32[384]{0:T(512)S(1)} %div.9), kind=kLoop, calls=%fused_computation.16 | loop fusion | flops 6291072 | bytes 12585984 | tf_op jit(solution)/shard_map/reduce_sum | solution.py:50
  203.0 69.6 %psum.60 = f32[384]{0:T(512)S(1)} all-reduce(f32[384]{0:T(512)S(1)} %multiply_reduce_fusion), channel_id=1, replica_groups=mesh['sub'=8,'grp'=16] {'sub','grp'}, use_global_device_ids=true, to_apply=%region_9.11 | all-reduce | flops 384 | bytes 3072 | tf_op jit(solution)/shard_map/psum | solution.py:50
  272.7 7.1 %fusion.21 = (bf16[4,1024,384]{2,1,0:T(8,128)(2,1)S(1)}, f32[4,1024,384]{2,1,0:T(8,128)}) fusion(f32[4,1024,384]{2,1,0:T(8,128)} %param.13, f32[384]{0:T(512)S(1)} %div.10, f32[4,1024,384]{2,0,1:T(4,128)} %scatter_fusion, f32[384]{0:T(512)S(1)} %div.9), kind=kLoop, calls=%fused_computation.58 | loop fusion | flops 7864320 | bytes 22023168 | tf_op jit(solution)/shard_map/convert_element_type | solution.py:22
  279.8 1.1 convert_bitcast_fusion
  281.5 1.4 fusion.22
  282.8 1.9 gather_fusion.3
  284.8 2.8 broadcast_select_fusion
  287.6 1.1 collective-permute-start.2
  288.6 2.8 slice.23
  292.5 78.0 %all-reduce.5.cloned.1.call-done = bf16[128,384]{1,0:T(8,128)(2,1)} async-done(((bf16[128,384]{1,0:T(8,128)(2,1)}), bf16[128,384]{1,0:T(8,128)(2,1)}) %all-reduce.5.cloned.1.call-update) | async-done | bytes 98320 | tf_op jit(solution)/shard_map/psum | solution.py:70
  370.5 1.2 convolution_bitcast_fusion
  372.0 3.5 subtract_convert_fusion
  375.5 2.6 copy.31
  378.1 3.3 gather_fusion.2
  381.4 3.1 subtract_convert_fusion.1
  384.5 2.7 copy.30
  387.2 5.1 %fusion.7 = f32[4,8,384,128]{2,3,1,0:T(8,128)} fusion(bf16[4,8,128,128]{3,2,1,0:T(8,128)(2,1)S(1)} %copy-done, bf16[4,4,128,384]{3,2,1,0:T(8,128)(2,1)S(1)} %bitcast.72, bf16[4,4,128,384]{3,2,1,0:T(8,128)(2,1)} %bitcast.74), kind=kOutput, calls=%fused_computation.22 | convolution fusion | flops 404226048 | bytes 10485760 | tf_op jit(solution)/shard_map/sfji,sfjr->sfir/dot_general | solution.py:45
  392.3 6.5 %copy.41 = f32[4,1024,384]{1,2,0:T(8,128)} copy(f32[4,1024,384]{2,1,0:T(8,128)} %bitcast.68) | data formatting | bytes 12582912 | tf_op jit(solution)/shard_map/reshape | solution.py:46
  398.8 12.4 %bitcast_add_fusion.1 = f32[4,1024,384]{1,2,0:T(8,128)} fusion(f32[4,1024,384]{1,2,0:T(8,128)} %copy.41, bf16[4,1024,384]{2,1,0:T(8,128)(2,1)} %copy-done.3, bf16[4,1024,1024]{2,1,0:T(8,128)(2,1)} %param.8), kind=kOutput, calls=%fused_computation.7 | convolution fusion | flops 3222798336 | bytes 24117248 | tf_op jit(solution)/shard_map/sij,sjr->sir/dot_general | solution.py:23
  411.2 7.7 %copy.34 = f32[4,1024,384]{2,0,1:T(4,128)} copy(f32[4,1024,384]{1,2,0:T(8,128)} %bitcast_add_fusion.1) | data formatting | bytes 12582912 | tf_op jit(solution)/shard_map/add | solution.py:46
  418.9 2.1 scatter_fusion.1
  420.9 5.3 %fusion = f32[384]{0:T(512)S(1)} fusion(f32[4,1024,384]{2,1,0:T(8,128)} %get-tuple-element.9, f32[4,1024,384]{2,0,1:T(4,128)} %scatter_fusion.1), kind=kLoop, calls=%fused_computation.9 | loop fusion | flops 3145344 | bytes 12584448 | tf_op jit(solution)/shard_map/reduce_sum | solution.py:74
  426.2 14.4 %psum.62 = f32[384]{0:T(512)S(1)} all-reduce(f32[384]{0:T(512)S(1)} %fusion), channel_id=1, replica_groups=mesh['sub'=8,'grp'=16] {'sub'}, use_global_device_ids=true, to_apply=%region_13.15 | all-reduce | flops 384 | bytes 3072 | tf_op jit(solution)/shard_map/psum | solution.py:74
  440.6 31.0 %psum.63 = f32[384]{0:T(512)S(1)} all-reduce(f32[384]{0:T(512)S(1)} %psum.62), channel_id=1, replica_groups=mesh['sub'=8,'grp'=16] {'grp'}, use_global_device_ids=true, to_apply=%region_14.16 | all-reduce | flops 384 | bytes 3072 | tf_op jit(solution)/shard_map/psum | solution.py:74
  471.7 8.0 %multiply_add_fusion = f32[4,1024,384]{2,1,0:T(8,128)} fusion(f32[4,1024,384]{2,1,0:T(8,128)} %get-tuple-element.9, f32[4,1024,384]{2,1,0:T(8,128)} %param.13, f32[384]{0:T(512)S(1)} %div.11, f32[384]{0:T(512)S(1)} %div.9), kind=kLoop, calls=%fused_computation.14 | loop fusion | flops 4718592 | bytes 18877440 | tf_op jit(solution)/shard_map/add | solution.py:77
  (47 shorter events, 5.0 us)
Async XLA Ops:
  6.5 5.6 %copy-start = (bf16[4,8,128,128]{3,2,1,0:T(8,128)(2,1)S(1)}, bf16[4,8,128,128]{3,2,1,0:T(8,128)(2,1)}, u32[]{:S(2)}) copy-start(bf16[4,8,128,128]{3,2,1,0:T(8,128)(2,1)} %param.9) | copy-start | bytes 3145732
  6.5 104.7 %all-reduce.3.cloned.1.call-start = ((), (), s32[]{:S(2)}) async-start(), calls=%async_computation | async-start | bytes 196608 | tf_op jit(solution)/shard_map/psum | solution.py:70
  12.2 1.7 copy-start.1
  13.8 3.0 copy-start.7
  15.4 97.3 %collective-permute-start = (bf16[16,128,384]{2,1,0:T(8,128)(2,1)}, bf16[16,128,384]{2,1,0:T(8,128)(2,1)}, u32[]{:S(2)}, u32[]{:S(2)}) collective-permute-start(bf16[16,128,384]{2,1,0:T(8,128)(2,1)} %bitcast.2), channel_id=1, source_target_pairs={{16,0},{32,16},{48,32},{64,48},{80,64},{96,80},{112,96},{0,112},{1... | collective-permute-start | bytes 4718600 | tf_op jit(solution)/shard_map/ppermute | solution.py:12
  18.1 9.2 %copy-start.6 = (s32[4,8]{1,0:T(4,128)S(1)}, s32[4,8]{1,0:T(4,128)}, u32[]{:S(2)}) copy-start(s32[4,8]{1,0:T(4,128)} %param.11) | copy-start | bytes 388
  18.1 93.1 %copy-start.5 = (f32[1,128,128]{2,1,0:T(8,128)S(1)}, f32[1,128,128]{2,1,0:T(8,128)}, u32[]{:S(2)}) copy-start(f32[1,128,128]{2,1,0:T(8,128)} %param.12) | copy-start | bytes 196612
  22.8 95.3 %collective-permute-start.1 = (bf16[16,128,384]{2,1,0:T(8,128)(2,1)}, bf16[16,128,384]{2,1,0:T(8,128)(2,1)}, u32[]{:S(2)}, u32[]{:S(2)}) collective-permute-start(bf16[16,128,384]{2,1,0:T(8,128)(2,1)} %broadcast_select_fusion.1), channel_id=1, source_target_pairs={{112,0},{0,16},{16,32},{32,48},{48,64},{64,80},{80,96},{96,112},{1... | collective-permute-start | bytes 4718600 | tf_op jit(solution)/shard_map/ppermute | solution.py:12
  28.3 342.2 %all-reduce.5.cloned.1.call-start = ((), (), s32[]{:S(2)}) async-start(), calls=%async_computation.1 | async-start | bytes 196608 | tf_op jit(solution)/shard_map/psum | solution.py:70
  118.2 3.6 slice-start
  120.7 2.3 slice-start.1
  120.7 3.2 copy-start.2
  279.8 1.7 copy-start.3
  287.6 84.4 %collective-permute-start.3 = (bf16[16,128,384]{1,2,0:T(8,128)(2,1)}, bf16[16,128,384]{1,2,0:T(8,128)(2,1)}, u32[]{:S(2)}, u32[]{:S(2)}) collective-permute-start(bf16[16,128,384]{1,2,0:T(8,128)(2,1)} %broadcast_select_fusion), channel_id=1, source_target_pairs={{112,0},{0,16},{16,32},{32,48},{48,64},{64,80},{80,96},{96,112},{1... | collective-permute-start | bytes 4718600 | tf_op jit(solution)/shard_map/ppermute | solution.py:12
  287.6 90.5 %collective-permute-start.2 = (bf16[16,128,384]{1,2,0:T(8,128)(2,1)}, bf16[16,128,384]{1,2,0:T(8,128)(2,1)}, u32[]{:S(2)}, u32[]{:S(2)}) collective-permute-start(bf16[16,128,384]{1,2,0:T(8,128)(2,1)} %bitcast.16), channel_id=1, source_target_pairs={{16,0},{32,16},{48,32},{64,48},{80,64},{96,80},{112,96},{0,112},{1... | collective-permute-start | bytes 4718600 | tf_op jit(solution)/shard_map/ppermute | solution.py:12
  384.5 2.7 copy-start.4
Sparse Core Ops, SparseCore 0:
  28.4 82.7 all-reduce.2
  292.6 77.8 all-reduce.4
